TPU v7x, 256 devices: a whole 4x4x8 slice. The times are simulated.
256 devices in a mesh: wide: 32 (over y, x, core), narrow: 8 (over z).
Axes of the slice: x: 4, y: 4, z: 8, core: 2. Of those that a mesh axis runs over, the one named last changes fastest.
Arguments:
- three_centre: float32 [128, 2048, 1024], P(None, 'wide', 'narrow'), may hold values from -6 to 6
- screen_mask: int32 [128, 16, 8], P('wide', None, 'narrow'), may hold values 0 or 1
- metric: bfloat16 [1024, 1024], P(None, 'narrow'), may hold values from -0.1875 to 0.1875
Outputs:
- contracted: float32 [128, 2048, 1024], P('wide', None, 'narrow')
All inputs are finite; a program needn't handle non-finite values. No bound on the sum of `screen_mask` on one device may be relied on, other than what follows from the above.
Results may differ from a plain program's by a relative error of at most 0.0029.
Values may be sent and summed in bfloat16 or wider, within the bound.
A program may use at most 64 MiB of HBM per device.

v0:
```python
import jax
import jax.numpy as jnp
from jax import lax
from jax.sharding import PartitionSpec as P


def per_device(three_centre, screen_mask, metric):
    nub_all = screen_mask.shape[1]
    auxb_local = screen_mask.shape[2]
    remapped = lax.all_to_all(
        three_centre.astype(jnp.bfloat16), "wide", split_axis=0, concat_axis=1, tiled=True
    ).astype(three_centre.dtype)
    mu_local, nu_all, aux_local = remapped.shape
    block_rows = nu_all // nub_all
    block_cols = aux_local // auxb_local
    blocks = remapped.reshape(mu_local, nub_all, block_rows, auxb_local, block_cols)
    weights = screen_mask[:, :, None, :, None].astype(jnp.float32)
    screened = (blocks * weights).reshape(mu_local, nu_all, aux_local).astype(jnp.bfloat16)
    initial = jnp.zeros((mu_local, nu_all, metric.shape[1]), jnp.float32)
    piece = lax.all_gather(screened, "narrow", axis=2, tiled=True)
    flat = piece.reshape(-1, piece.shape[2])
    product = jnp.dot(flat, metric, preferred_element_type=jnp.float32)
    return product.reshape(initial.shape)


def solution(mesh):
    in_specs = (P(None, "wide", "narrow"), P("wide", None, "narrow"), P(None, "narrow"))
    out_specs = P("wide", None, "narrow")
    return jax.shard_map(
        per_device, mesh=mesh, in_specs=in_specs, out_specs=out_specs, check_vma=False
    )
```

profile of v0, /device:TPU:2, one launch (start us, length us, event | category | flops | bytes accessed | tf_op | source)
XLA Modules:
  0.0 246.3 jit_solution(7557963478260871547)
XLA Ops:
  6.5 0.0 copy-start
  6.5 0.0 copy-start.1
  6.5 4.1 %convert_element_type.32 = bf16[128,64,128]{2,1,0:T(8,128)(2,1)} convert(f32[128,64,128]{2,1,0:T(8,128)} %param.3) | non-fusion elementwise | flops 1048576 | bytes 6291456 | tf_op jit(solution)/shard_map/convert_element_type | solution.py:11
  10.6 7.6 %all-to-all-start = ((bf16[128,64,128]{2,1,0:T(8,128)(2,1)}), bf16[128,64,128]{2,1,0:T(8,128)(2,1)S(1)}, u32[]{:S(2)}, u32[]{:S(2)}) async-start(bf16[128,64,128]{2,1,0:T(8,128)(2,1)} %convert_element_type.32), calls=%async_computation | async-start | bytes 4194304 | tf_op jit(solution)/shard_map/all_to_all | solution.py:10
  18.2 0.0 all-gather.2.cloned.1.call-start
  18.3 0.0 copy-done.1
  18.3 0.1 broadcast_bitcast_fusion
  18.4 27.7 %all-to-all-done = bf16[128,64,128]{2,1,0:T(8,128)(2,1)S(1)} async-done(((bf16[128,64,128]{2,1,0:T(8,128)(2,1)}), bf16[128,64,128]{2,1,0:T(8,128)(2,1)S(1)}, u32[]{:S(2)}, u32[]{:S(2)}) %all-to-all-start) | async-done | bytes 2097184 | tf_op jit(solution)/shard_map/all_to_all | solution.py:10
  46.1 0.4 copy.4
  46.6 2.5 %fusion = bf16[4,2048,128]{2,1,0:T(8,128)(2,1)} fusion(f32[32,4,64,128]{3,2,0,1:T(8,128)S(1)} %copy.4, f32[4,2048]{1,0:T(4,128)S(1)} %bitcast.19), kind=kLoop, calls=%fused_computation.1 | loop fusion | flops 2097152 | bytes 6324224 | tf_op jit(solution)/shard_map/convert_element_type | solution.py:18
  49.1 0.0 all-gather.2.cloned.1.call-update
  49.1 180.2 %all-gather.2.cloned.1.call-done = bf16[4,2048,1024]{2,1,0:T(8,128)(2,1)} async-done(((bf16[4,2048,128]{2,1,0:T(8,128)(2,1)}), bf16[4,2048,1024]{2,1,0:T(8,128)(2,1)}) %all-gather.2.cloned.1.call-update) | async-done | bytes 16777232 | tf_op jit(solution)/shard_map/all_gather | solution.py:20
  229.3 0.0 copy-done
  229.3 10.1 %fusion.1 = f32[4,2048,128]{2,1,0:T(8,128)} fusion(bf16[4,2048,1024]{2,1,0:T(8,128)(2,1)} %all-gather.2.cloned.1.call-done, bf16[1024,128]{1,0:T(8,128)(2,1)S(1)} %copy-done), kind=kOutput, calls=%fused_computation.2 | convolution fusion | flops 2147483648 | bytes 21233664 | tf_op jit(solution)/shard_map/dot_general | solution.py:22
  (2 shorter events, 0.0 us)
Async XLA Ops:
  6.5 222.8 %copy-start = (bf16[1024,128]{1,0:T(8,128)(2,1)S(1)}, bf16[1024,128]{1,0:T(8,128)(2,1)}, u32[]{:S(2)}) copy-start(bf16[1024,128]{1,0:T(8,128)(2,1)} %param.5) | copy-start | bytes 786436
  6.5 11.7 %copy-start.1 = (s32[4,16,1]{1,2,0:T(1,128)S(1)}, s32[4,16,1]{1,2,0:T(1,128)}, u32[]{:S(2)}) copy-start(s32[4,16,1]{1,2,0:T(1,128)} %param.4) | copy-start | bytes 772
  10.6 35.5 %all-to-all-start = ((bf16[128,64,128]{2,1,0:T(8,128)(2,1)}), bf16[128,64,128]{2,1,0:T(8,128)(2,1)S(1)}, u32[]{:S(2)}, u32[]{:S(2)}) async-start(bf16[128,64,128]{2,1,0:T(8,128)(2,1)} %convert_element_type.32), calls=%async_computation | async-start | bytes 4194304 | tf_op jit(solution)/shard_map/all_to_all | solution.py:10
  18.2 211.1 %all-gather.2.cloned.1.call-start = ((), (), s32[]{:S(2)}) async-start(), calls=%async_computation.1 | async-start | bytes 18874368 | tf_op jit(solution)/shard_map/all_gather | solution.py:20
Sparse Core Ops, SparseCore 0:
  49.2 180.0 all-gather.1
where the time goes:
time: 246 us
  waiting for transfers between devices  208 us (85%)
  between operations  13.4 us (5%)
  matrix products  10.1 us (4%)
  starting transfers between devices  7.66 us (3%)
  other arithmetic  6.57 us (3%)
    all_gather x1, waiting for transfers between devices, per_device(): piece = lax.all_gather(screened, 'narrow', axis=2, tiled=True)  180 us
    all_to_all x1, waiting for transfers between devices, per_device(): lax.all_to_all(three_centre.astype(jnp.bfloat16), 'wide', split_axis=0, c...  27.7 us
    dot_general x1, matrix products, per_device(): product = jnp.dot(flat, metric, preferred_element_type=jnp.float32)  10.1 us
    all_to_all x1, starting transfers between devices, per_device(): lax.all_to_all(three_centre.astype(jnp.bfloat16), 'wide', split_axis=0, c...  7.62 us
  transfers between devices with their start and end apart: 2, of which 2 were waited for; matrix products, arithmetic and copies ran while one was open for 0% of the time, Pallas kernels for 0%

commit v1 on v0

--- a/solution.py
+++ b/solution.py
@@ -17,7 +17,9 @@
     weights = screen_mask[:, :, None, :, None].astype(jnp.float32)
     screened = (blocks * weights).reshape(mu_local, nu_all, aux_local).astype(jnp.bfloat16)
     initial = jnp.zeros((mu_local, nu_all, metric.shape[1]), jnp.float32)
-    piece = lax.all_gather(screened, "narrow", axis=2, tiled=True)
+    piece = jnp.concatenate(
+        lax.all_to_all(jnp.stack([screened] * lax.axis_size("narrow")), "narrow", 0, 0), axis=2
+    )
     flat = piece.reshape(-1, piece.shape[2])
     product = jnp.dot(flat, metric, preferred_element_type=jnp.float32)
     return product.reshape(initial.shape)

time: 246 us -> 425 us (1.73)
  blocking collectives: 0 us -> 374 us
  waiting for transfers between devices: 208 us -> 27.8 us
  between operations: 13.4 us -> 0.07 us
    all_to_all x0 -> x1, blocking collectives: none -> 374 us  [per_device(): lax.all_to_all(jnp.stack([screened] * lax.axis_size('narrow')), 'narrow',...]
    all_gather x1 -> x0, waiting for transfers between devices: 180 us -> none  [per_device(): piece = lax.all_gather(screened, 'narrow', axis=2, tiled=True)]
  transfers between devices with their start and end apart: 2 -> 1, of which waited for: 2 -> 1; matrix products, arithmetic and copies ran while one was open for 0% -> 0% of each run, Pallas kernels for 0% -> 0%
where the time goes in v1:
time: 425 us; the launch traced here: 424 us
  blocking collectives  374 us (88%)
  waiting for transfers between devices  27.8 us (7%)
  starting transfers between devices  7.62 us (2%)
  matrix products  6.1 us (1%)
  other arithmetic  5.97 us (1%)
    all_to_all x1, blocking collectives, per_device(): lax.all_to_all(jnp.stack([screened] * lax.axis_size('narrow')), 'narrow',...  374 us
    all_to_all x1, waiting for transfers between devices, per_device(): lax.all_to_all(three_centre.astype(jnp.bfloat16), 'wide', split_axis=0, c...  27.8 us
  transfers between devices with their start and end apart: 1, of which 1 were waited for; matrix products, arithmetic and copies ran while one was open for 0% of the time, Pallas kernels for 0%

profile of v1, /device:TPU:2, one launch (start us, length us, event | category | flops | bytes accessed | tf_op | source)
XLA Modules:
  0.0 424.2 jit_solution(14761576869081528431)
XLA Ops:
  0.0 0.0 copy-start
  0.0 0.0 copy-start.1
  0.0 4.1 convert_element_type.36
  4.1 7.6 %all-to-all-start = ((bf16[128,64,128]{2,1,0:T(8,128)(2,1)}), bf16[128,64,128]{2,1,0:T(8,128)(2,1)S(1)}, u32[]{:S(2)}, u32[]{:S(2)}) async-start(bf16[128,64,128]{2,1,0:T(8,128)(2,1)} %convert_element_type.36), calls=%async_computation | async-start | bytes 4194304 | tf_op jit(solution)/shard_map/all_to_all | solution.py:10
  11.7 0.0 copy-done.1
  11.7 0.1 broadcast_bitcast_fusion
  11.8 27.8 %all-to-all-done = bf16[128,64,128]{2,1,0:T(8,128)(2,1)S(1)} async-done(((bf16[128,64,128]{2,1,0:T(8,128)(2,1)}), bf16[128,64,128]{2,1,0:T(8,128)(2,1)S(1)}, u32[]{:S(2)}, u32[]{:S(2)}) %all-to-all-start) | async-done | bytes 2097184 | tf_op jit(solution)/shard_map/all_to_all | solution.py:10
  39.6 0.5 convert_bitcast_fusion
  40.1 0.6 copy.5
  40.7 1.4 fusion.3
  42.1 2.3 stack.2
  44.4 373.7 %all_to_all.14 = bf16[8,4,2048,128]{3,2,1,0:T(8,128)(2,1)S(1)} all-to-all(bf16[8,4,2048,128]{3,2,1,0:T(8,128)(2,1)S(1)} %stack.2), channel_id=1, replica_groups=mesh['wide'=32,'narrow'=8] {'narrow'}, dimensions={0} | all-to-all | bytes 33554432 | tf_op jit(solution)/shard_map/all_to_all | solution.py:21
  418.1 0.0 copy-done
  418.1 6.1 %fusion = f32[4,2048,128]{2,1,0:T(8,128)} fusion(bf16[1024,128]{1,0:T(8,128)(2,1)S(1)} %copy-done, bf16[8,4,2048,128]{3,2,1,0:T(8,128)(2,1)S(1)} %all_to_all.14), kind=kOutput, calls=%fused_computation | convolution fusion | flops 2147483648 | bytes 21233664 | tf_op jit(solution)/shard_map/dot_general | solution.py:24
  (2 shorter events, 0.0 us)
Async XLA Ops:
  0.0 418.1 %copy-start = (bf16[1024,128]{1,0:T(8,128)(2,1)S(1)}, bf16[1024,128]{1,0:T(8,128)(2,1)}, u32[]{:S(2)}) copy-start(bf16[1024,128]{1,0:T(8,128)(2,1)} %param.5) | copy-start | bytes 786436
  0.0 11.7 %copy-start.1 = (s32[4,16,1]{1,2,0:T(1,128)S(1)}, s32[4,16,1]{1,2,0:T(1,128)}, u32[]{:S(2)}) copy-start(s32[4,16,1]{1,2,0:T(1,128)} %param.4) | copy-start | bytes 772
  4.1 35.5 %all-to-all-start = ((bf16[128,64,128]{2,1,0:T(8,128)(2,1)}), bf16[128,64,128]{2,1,0:T(8,128)(2,1)S(1)}, u32[]{:S(2)}, u32[]{:S(2)}) async-start(bf16[128,64,128]{2,1,0:T(8,128)(2,1)} %convert_element_type.36), calls=%async_computation | async-start | bytes 4194304 | tf_op jit(solution)/shard_map/all_to_all | solution.py:10
